TPU v7x, 128 devices: a whole 4x4x4 slice. The times are simulated.
128 devices in a mesh: seq: 16 (over x_lo, z, core), tensor: 8 (over y, x_hi).
Axes of the slice: x: 4 (x_hi: 2, x_lo: 2; x = x_hi * 2 + x_lo), y: 4, z: 4, core: 2. Of those that a mesh axis runs over, the one named last changes fastest.
Arguments:
- tokens: bfloat16 [2048, 8192], P('seq', 'tensor'), may hold values from -2000 to 2000
- cotangent: bfloat16 [2048, 8192], P('seq', 'tensor'), may hold values from -6 to 6
- gain: float32 [8192], P('tensor'), may hold values from 0.25 to 1.75
- w_gate: bfloat16 [8192, 14336], P('tensor', 'seq'), may hold values from -0.0625 to 0.0625
- w_up: bfloat16 [8192, 14336], P('tensor', 'seq'), may hold values from -0.0625 to 0.0625
- w_down: bfloat16 [14336, 8192], P('seq', 'tensor'), may hold values from -0.046875 to 0.046875
- probe: bfloat16 [8192, 14336], P('tensor', 'seq'), may hold values from -1 to 1, as said below
Outputs:
- hessian_probe: float32 [8192, 14336], P('tensor', 'seq')
Inputs may be any that keep to these rules, and one draw needn't show every extreme that they name: `probe`: every entry is +1 or -1.
All inputs are finite; a program needn't handle non-finite values.
Results may differ from a plain program's by a relative error of at most 0.024.
Values may be sent and summed in bfloat16 or wider, within the bound.
No kernel may reach another device: no remote copies, remote signals or barrier semaphores. Data moves between devices by JAX's collectives and lax.ppermute only.
A program may use at most 128 MiB of HBM per device.

v0:
```python
import jax
import jax.numpy as jnp
from jax import lax
from jax.sharding import PartitionSpec as P

D = 8192
epsilon = 1e-05


def second_factor(pre_gate, pre_up, tangent, upstream):
    sigmoid_gate = jax.nn.sigmoid(pre_gate)
    curvature = sigmoid_gate * (1.0 - sigmoid_gate) * (2.0 + pre_gate * (1.0 - 2.0 * sigmoid_gate))
    return (upstream * pre_up * curvature * tangent).astype(jnp.bfloat16)


def body(tokens, cotangent, gain, w_gate, w_up, w_down, probe):
    gathered, upstream_rows = (
        lax.all_gather(tokens, "seq", axis=0, tiled=True),
        lax.all_gather(cotangent, "seq", axis=0, tiled=True),
    )
    values = gathered.astype(jnp.float32)
    squares = lax.psum(jnp.sum(values * values, axis=1), "tensor")
    inverse = lax.rsqrt(squares / D + epsilon)
    normed = (values * inverse[:, None] * gain[None, :]).astype(jnp.bfloat16)
    total_tokens = normed.shape[0]
    unit_count = w_gate.shape[1]
    norm_block = normed
    outputs = [
        jnp.dot(norm_block, weight, preferred_element_type=jnp.float32)
        for weight in (w_gate, w_up, probe)
    ]
    outputs.append(
        lax.dot_general(
            upstream_rows, w_down, (((1,), (1,)), ((), ())), preferred_element_type=jnp.float32
        )
    )
    summed = lax.psum_scatter(
        jnp.concatenate(outputs, axis=1).astype(jnp.bfloat16),
        "tensor",
        scatter_dimension=0,
        tiled=True,
    ).astype(jnp.float32)
    second = second_factor(
        summed[:, :unit_count],
        summed[:, unit_count : 2 * unit_count],
        summed[:, 2 * unit_count : 3 * unit_count],
        summed[:, 3 * unit_count :],
    )
    norm_block = normed
    product = lax.dot_general(
        norm_block,
        lax.all_gather(second, "tensor", axis=0, tiled=True),
        (((0,), (0,)), ((), ())),
        preferred_element_type=jnp.float32,
    )
    return product / total_tokens


def solution(mesh):
    return jax.shard_map(
        body,
        mesh=mesh,
        in_specs=(
            P("seq", "tensor"),
            P("seq", "tensor"),
            P("tensor"),
            P("tensor", "seq"),
            P("tensor", "seq"),
            P("seq", "tensor"),
            P("tensor", "seq"),
        ),
        out_specs=P("tensor", "seq"),
        check_vma=False,
    )
```

profile of v0, /device:TPU:0, one launch (start us, length us, event | category | flops | bytes accessed | tf_op | source)
XLA Modules:
  0.0 385.9 jit_solution(4910168652188962719)
XLA Ops:
  6.5 0.0 copy-start
  6.5 0.0 copy-start.7
  6.5 0.0 all-gather.4.cloned.1.call-start
  6.5 0.7 all-gather.4.cloned.1.call-update
  7.3 0.0 all-gather.6.cloned.1.call-start
  7.3 0.7 all-gather.6.cloned.1.call-update
  8.0 0.0 reduce-scatter.2.cloned.1.call-start
  8.1 40.8 %all-gather.4.cloned.1.call-done = bf16[2048,1024]{1,0:T(8,128)(2,1)} async-done(((bf16[128,1024]{1,0:T(8,128)(2,1)}), bf16[2048,1024]{1,0:T(8,128)(2,1)}) %all-gather.4.cloned.1.call-update) | async-done | bytes 4194320 | tf_op jit(solution)/shard_map/all_gather | solution.py:18
  48.9 3.1 fusion
  52.0 24.9 %psum.7 = f32[2048]{0:T(1024)S(1)} all-reduce(f32[2048]{0:T(1024)S(1)} %fusion), channel_id=1, replica_groups=mesh['seq'=16,'tensor'=8] {'tensor'}, use_global_device_ids=true, to_apply=%region_1.0 | all-reduce | flops 2048 | bytes 16384 | tf_op jit(solution)/shard_map/psum | solution.py:22
  76.9 0.0 copy-done
  76.9 0.0 copy-done.7
  76.9 0.0 copy-start.1
  77.0 0.0 copy-start.5
  77.0 8.5 %convolution_convert_fusion.2 = bf16[2048,896]{0,1:T(8,128)(2,1)} fusion(bf16[1024,896]{1,0:T(8,128)(2,1)S(1)} %copy-done, bf16[2048,1024]{1,0:T(8,128)(2,1)} %all-gather.4.cloned.1.call-done, f32[1024]{0:T(1024)S(1)} %copy-done.7, f32[2048]{0:T(1024)S(1)} %add_rsqrt_fusion), kind=kOutput, calls=%fused_computation.8 | convolution fusion | flops 3768320000 | bytes 9711616 | tf_op jit(solution)/shard_map/dot_general | solution.py:29
  85.4 0.0 copy-done.1
  85.4 0.0 copy-done.5
  85.4 0.0 copy-start.6
  85.4 6.0 %convolution_convert_fusion.1 = bf16[2048,896]{0,1:T(8,128)(2,1)} fusion(bf16[1024,896]{1,0:T(8,128)(2,1)S(1)} %copy-done.5, bf16[2048,1024]{1,0:T(8,128)(2,1)S(1)} %copy-done.1, f32[1024]{0:T(1024)S(1)} %copy-done.7, f32[2048]{0:T(1024)S(1)} %add_rsqrt_fusion), kind=kOutput, calls=%fused_computation.7 | convolution fusion | flops 3768320000 | bytes 9711616 | tf_op jit(solution)/shard_map/dot_general | solution.py:29
  91.5 0.0 copy-done.6
  91.5 5.9 %convolution_convert_fusion.3 = bf16[2048,896]{0,1:T(8,128)(2,1)} fusion(bf16[1024,896]{1,0:T(8,128)(2,1)S(1)} %copy-done.6, bf16[2048,1024]{1,0:T(8,128)(2,1)S(1)} %copy-done.1, f32[1024]{0:T(1024)S(1)} %copy-done.7, f32[2048]{0:T(1024)S(1)} %add_rsqrt_fusion), kind=kOutput, calls=%fused_computation.9 | convolution fusion | flops 3768320000 | bytes 9711616 | tf_op jit(solution)/shard_map/dot_general | solution.py:29
  97.3 0.0 all-gather.6.cloned.1.call-done
  97.4 0.0 copy-start.2
  97.4 0.0 copy-start.3
  97.4 0.0 copy-start.4
  97.4 6.9 %convolution_convert_fusion = bf16[2048,896]{0,1:T(8,128)(2,1)S(1)} fusion(bf16[2048,1024]{1,0:T(8,128)(2,1)} %all-gather.6.cloned.1.call-done, bf16[896,1024]{1,0:T(8,128)(2,1)} %param.12), kind=kOutput, calls=%fused_computation.6 | convolution fusion | flops 3759931392 | bytes 9699328 | tf_op jit(solution)/shard_map/dot_general | solution.py:33
  104.3 0.0 copy-done.2
  104.3 0.0 copy-done.3
  104.3 0.0 copy-done.4
  104.3 31.3 %pad_maximum_fusion = bf16[2048,3584]{0,1:T(8,128)(2,1)} fusion(bf16[2048,896]{0,1:T(8,128)(2,1)S(1)} %convolution_convert_fusion, bf16[2048,896]{0,1:T(8,128)(2,1)S(1)} %copy-done.3, bf16[2048,896]{0,1:T(8,128)(2,1)S(1)} %copy-done.2, bf16[2048,896]{0,1:T(8,128)(2,1)S(1)} %copy-done.4), kind=kLoop, calls=%fused_computation | loop fusion | flops 58720256 | bytes 29360128 | tf_op jit(solution)/shard_map/concatenate | solution.py:38
  135.6 0.0 reduce-scatter.2.cloned.1.call-update
  135.6 0.0 all-gather.8.cloned.1.call-start
  135.7 164.5 %reduce-scatter.2.cloned.1.call-done = bf16[256,3584]{0,1:T(8,128)(2,1)} async-done(((bf16[2048,3584]{0,1:T(8,128)(2,1)}), bf16[256,3584]{0,1:T(8,128)(2,1)}) %reduce-scatter.2.cloned.1.call-update) | async-done | bytes 1835024 | tf_op jit(solution)/shard_map/reduce_scatter | solution.py:37
  300.1 1.8 convert_element_type.15
  301.9 1.2 fusion.6
  303.1 0.0 all-gather.8.cloned.1.call-update
  303.2 66.1 %all-gather.8.cloned.1.call-done = bf16[2048,896]{0,1:T(8,128)(2,1)} async-done(((bf16[256,896]{0,1:T(8,128)(2,1)}), bf16[2048,896]{0,1:T(8,128)(2,1)}) %all-gather.8.cloned.1.call-update) | async-done | bytes 3670032 | tf_op jit(solution)/shard_map/all_gather | solution.py:52
  369.3 10.1 %convolution_multiply_fusion = f32[1024,896]{1,0:T(8,128)} fusion(bf16[2048,896]{0,1:T(8,128)(2,1)} %all-gather.8.cloned.1.call-done, bf16[2048,1024]{1,0:T(8,128)(2,1)} %all-gather.4.cloned.1.call-done, f32[1024]{0:T(1024)S(1)} %copy-done.7, f32[2048]{0:T(1024)S(1)} %add_rsqrt_fusion), kind=kOutput, calls=%fused_computation.10 | convolution fusion | flops 3767402496 | bytes 11546624 | tf_op jit(solution)/shard_map/dot_general | solution.py:50
  (1 shorter events, 0.0 us)
Async XLA Ops:
  6.5 70.4 %copy-start = (bf16[1024,896]{1,0:T(8,128)(2,1)S(1)}, bf16[1024,896]{1,0:T(8,128)(2,1)}, u32[]{:S(2)}) copy-start(bf16[1024,896]{1,0:T(8,128)(2,1)} %param.11) | copy-start | bytes 5505028
  6.5 70.4 %copy-start.7 = (f32[1024]{0:T(1024)S(1)}, f32[1024]{0:T(1024)}, u32[]{:S(2)}) copy-start(f32[1024]{0:T(1024)} %param.9) | copy-start | bytes 12292
  6.5 42.4 %all-gather.4.cloned.1.call-start = ((), (), s32[]{:S(2)}) async-start(), calls=%async_computation.1 | async-start | bytes 4456448 | tf_op jit(solution)/shard_map/all_gather | solution.py:18
  7.3 90.1 %all-gather.6.cloned.1.call-start = ((), (), s32[]{:S(2)}) async-start(), calls=%async_computation.2 | async-start | bytes 4456448 | tf_op jit(solution)/shard_map/all_gather | solution.py:19
  8.0 292.1 %reduce-scatter.2.cloned.1.call-start = ((), (), s32[]{:S(2)}) async-start(), calls=%async_computation.3 | async-start | bytes 16515072 | tf_op jit(solution)/shard_map/reduce_scatter | solution.py:37
  76.9 8.5 %copy-start.1 = (bf16[2048,1024]{1,0:T(8,128)(2,1)S(1)}, bf16[2048,1024]{1,0:T(8,128)(2,1)}, u32[]{:S(2)}) copy-start(bf16[2048,1024]{1,0:T(8,128)(2,1)} %all-gather.4.cloned.1.call-done) | copy-start | bytes 12582916
  77.0 8.5 %copy-start.5 = (bf16[1024,896]{1,0:T(8,128)(2,1)S(1)}, bf16[1024,896]{1,0:T(8,128)(2,1)}, u32[]{:S(2)}) copy-start(bf16[1024,896]{1,0:T(8,128)(2,1)} %param.13) | copy-start | bytes 5505028
  85.4 6.0 %copy-start.6 = (bf16[1024,896]{1,0:T(8,128)(2,1)S(1)}, bf16[1024,896]{1,0:T(8,128)(2,1)}, u32[]{:S(2)}) copy-start(bf16[1024,896]{1,0:T(8,128)(2,1)} %param.10) | copy-start | bytes 5505028
  97.4 6.9 %copy-start.2 = (bf16[2048,896]{0,1:T(8,128)(2,1)S(1)}, bf16[2048,896]{0,1:T(8,128)(2,1)}, u32[]{:S(2)}) copy-start(bf16[2048,896]{0,1:T(8,128)(2,1)} %convolution_convert_fusion.2) | copy-start | bytes 11010052
  97.4 6.9 %copy-start.3 = (bf16[2048,896]{0,1:T(8,128)(2,1)S(1)}, bf16[2048,896]{0,1:T(8,128)(2,1)}, u32[]{:S(2)}) copy-start(bf16[2048,896]{0,1:T(8,128)(2,1)} %convolution_convert_fusion.1) | copy-start | bytes 11010052
  97.4 6.9 %copy-start.4 = (bf16[2048,896]{0,1:T(8,128)(2,1)S(1)}, bf16[2048,896]{0,1:T(8,128)(2,1)}, u32[]{:S(2)}) copy-start(bf16[2048,896]{0,1:T(8,128)(2,1)} %convolution_convert_fusion.3) | copy-start | bytes 11010052
  135.6 233.7 %all-gather.8.cloned.1.call-start = ((), (), s32[]{:S(2)}) async-start(), calls=%async_computation.4 | async-start | bytes 4128768 | tf_op jit(solution)/shard_map/all_gather | solution.py:52
Sparse Core Ops, SparseCore 0:
  9.0 39.8 all-gather.3
  50.6 37.3 all-gather.5
  135.7 164.3 reduce-scatter.1
  303.3 65.9 all-gather.7
where the time goes:
time: 386 us
  waiting for transfers between devices  273 us (71%)
  other arithmetic  37.4 us (10%)
  matrix products  37.4 us (10%)
  blocking collectives  24.9 us (6%)
  between operations  13.2 us (3%)
    reduce_scatter x1, waiting for transfers between devices, body(): lax.psum_scatter(jnp.concatenate(outputs, axis=1).astype(jnp.bfloat16), '...  164 us
    all_gather x1, waiting for transfers between devices, body(): lax.all_gather(second, 'tensor', axis=0, tiled=True)  66.1 us
    all_gather x1, waiting for transfers between devices, body(): lax.all_gather(tokens, 'seq', axis=0, tiled=True)  40.8 us
    concatenate x1, other arithmetic, body(): jnp.concatenate(outputs, axis=1).astype(jnp.bfloat16)  31.3 us
    psum x1, blocking collectives, body(): squares = lax.psum(jnp.sum(values * values, axis=1), 'tensor')  24.9 us
    dot_general x3, matrix products, body(): jnp.dot(norm_block, weight, preferred_element_type=jnp.float32)  20.4 us
    dot_general x1, matrix products, body(): lax.dot_general(norm_block, lax.all_gather(second, 'tensor', axis=0, tile...  10.1 us
  transfers between devices with their start and end apart: 4, of which 3 were waited for; matrix products, arithmetic and copies ran while one was open for 6% of the time, Pallas kernels for 0%

commit v1 on v0

--- a/solution.py
+++ b/solution.py
@@ -15,7 +15,12 @@
 
 def body(tokens, cotangent, gain, w_gate, w_up, w_down, probe):
     gathered, upstream_rows = (
-        lax.all_gather(tokens, "seq", axis=0, tiled=True),
+        jnp.concatenate(
+            lax.all_to_all(
+                jnp.stack([tokens for _ in range(lax.psum(1, "seq"))], axis=0), "seq", 0, 0
+            ),
+            0,
+        ),
         lax.all_gather(cotangent, "seq", axis=0, tiled=True),
     )
     values = gathered.astype(jnp.float32)

time: 386 us -> 417 us (1.080)
  blocking collectives: 24.9 us -> 98.9 us
  waiting for transfers between devices: 273 us -> 230 us
  matrix products: 37.4 us -> 33.2 us
    all_to_all x0 -> x1, blocking collectives: none -> 74.3 us  [body(): lax.all_to_all(jnp.stack([tokens for _ in range(lax.psum(1, 'seq'))], axi...]
    all_gather x1 -> x0, waiting for transfers between devices: 40.8 us -> none  [body(): lax.all_gather(tokens, 'seq', axis=0, tiled=True)]
  transfers between devices with their start and end apart: 4 -> 3, of which waited for: 3 -> 2; matrix products, arithmetic and copies ran while one was open for 6% -> 5% of each run, Pallas kernels for 0% -> 0%
where the time goes in v1:
time: 417 us
  waiting for transfers between devices  230 us (55%)
  blocking collectives  98.9 us (24%)
  other arithmetic  37.9 us (9%)
  matrix products  33.2 us (8%)
  between operations  13.2 us (3%)
    reduce_scatter x1, waiting for transfers between devices, body(): lax.psum_scatter(jnp.concatenate(outputs, axis=1).astype(jnp.bfloat16), '...  163 us
    all_to_all x1, blocking collectives, body(): lax.all_to_all(jnp.stack([tokens for _ in range(lax.psum(1, 'seq'))], axi...  74.3 us
    all_gather x1, waiting for transfers between devices, body(): lax.all_gather(second, 'tensor', axis=0, tiled=True)  66.2 us
    concatenate x1, other arithmetic, body(): jnp.concatenate(outputs, axis=1).astype(jnp.bfloat16)  31.2 us
    psum x1, blocking collectives, body(): squares = lax.psum(jnp.sum(values * values, axis=1), 'tensor')  24.6 us
    dot_general x3, matrix products, body(): jnp.dot(norm_block, weight, preferred_element_type=jnp.float32)  16.4 us
    dot_general x1, matrix products, body(): lax.dot_general(norm_block, lax.all_gather(second, 'tensor', axis=0, tile...  9.81 us
  transfers between devices with their start and end apart: 3, of which 2 were waited for; matrix products, arithmetic and copies ran while one was open for 5% of the time, Pallas kernels for 0%

profile of v1, /device:TPU:0, one launch (start us, length us, event | category | flops | bytes accessed | tf_op | source)
XLA Modules:
  0.0 416.7 jit_solution(6610163469404868983)
XLA Ops:
  6.5 0.0 copy-start
  6.5 0.0 all-gather.3.cloned.1.call-start
  6.5 0.7 all-gather.3.cloned.1.call-update
  7.3 0.0 reduce-scatter.2.cloned.1.call-start
  7.3 1.5 stack.2
  8.8 74.3 %all_to_all.5 = bf16[16,128,1024]{2,1,0:T(8,128)(2,1)S(1)} all-to-all(bf16[16,128,1024]{2,1,0:T(8,128)(2,1)S(1)} %stack.2), channel_id=1, replica_groups=mesh['seq'=16,'tensor'=8] {'seq'}, dimensions={0} | all-to-all | bytes 8388608 | tf_op jit(solution)/shard_map/all_to_all | solution.py:19
  83.1 0.0 copy-start.2
  83.1 2.0 copy-done.2
  85.1 0.0 copy-start.7
  85.1 0.9 multiply_reduce_fusion
  86.0 24.6 %psum.7 = f32[2048]{0:T(1024)S(1)} all-reduce(f32[2048]{0:T(1024)S(1)} %bitcast.17), channel_id=1, replica_groups=mesh['seq'=16,'tensor'=8] {'tensor'}, use_global_device_ids=true, to_apply=%region_1.0 | all-reduce | flops 2048 | bytes 16384 | tf_op jit(solution)/shard_map/psum | solution.py:27
  110.5 0.0 copy-done.7
  110.6 2.8 fusion.1
  113.4 0.0 copy-done
  113.4 0.0 copy-start.3
  113.4 0.0 copy-start.8
  113.4 5.5 %convolution_convert_fusion.1 = bf16[2048,896]{0,1:T(8,128)(2,1)} fusion(bf16[2048,1024]{1,0:T(8,128)(2,1)S(1)} %fusion.1, bf16[1024,896]{1,0:T(8,128)(2,1)S(1)} %copy-done), kind=kOutput, calls=%fused_computation.6 | convolution fusion | flops 3759931392 | bytes 9699328 | tf_op jit(solution)/shard_map/dot_general | solution.py:34
  118.9 0.0 copy-done.8
  118.9 0.0 copy-start.9
  118.9 5.5 %convolution_convert_fusion.2 = bf16[2048,896]{0,1:T(8,128)(2,1)} fusion(bf16[2048,1024]{1,0:T(8,128)(2,1)S(1)} %fusion.1, bf16[1024,896]{1,0:T(8,128)(2,1)S(1)} %copy-done.8), kind=kOutput, calls=%fused_computation.7 | convolution fusion | flops 3759931392 | bytes 9699328 | tf_op jit(solution)/shard_map/dot_general | solution.py:34
  124.4 0.0 copy-done.3
  124.4 0.0 copy-done.9
  124.4 5.5 %convolution_convert_fusion.3 = bf16[2048,896]{0,1:T(8,128)(2,1)} fusion(bf16[2048,1024]{1,0:T(8,128)(2,1)S(1)} %fusion.1, bf16[1024,896]{1,0:T(8,128)(2,1)S(1)} %copy-done.9), kind=kOutput, calls=%fused_computation.8 | convolution fusion | flops 3759931392 | bytes 9699328 | tf_op jit(solution)/shard_map/dot_general | solution.py:34
  129.8 0.0 all-gather.3.cloned.1.call-done
  129.8 0.0 copy-start.4
  129.8 0.0 copy-start.5
  129.9 0.0 copy-start.6
  129.9 6.9 %convolution_convert_fusion = bf16[2048,896]{0,1:T(8,128)(2,1)S(1)} fusion(bf16[2048,1024]{1,0:T(8,128)(2,1)} %all-gather.3.cloned.1.call-done, bf16[896,1024]{1,0:T(8,128)(2,1)} %param.12), kind=kOutput, calls=%fused_computation.5 | convolution fusion | flops 3759931392 | bytes 9699328 | tf_op jit(solution)/shard_map/dot_general | solution.py:38
  136.8 0.0 copy-done.4
  136.8 0.0 copy-done.5
  136.8 0.0 copy-done.6
  136.8 31.2 %pad_maximum_fusion = bf16[2048,3584]{0,1:T(8,128)(2,1)} fusion(bf16[2048,896]{0,1:T(8,128)(2,1)S(1)} %convolution_convert_fusion, bf16[2048,896]{0,1:T(8,128)(2,1)S(1)} %copy-done.4, bf16[2048,896]{0,1:T(8,128)(2,1)S(1)} %copy-done.5, bf16[2048,896]{0,1:T(8,128)(2,1)S(1)} %copy-done.6), kind=kLoop, calls=%fused_computation | loop fusion | flops 58720256 | bytes 29360128 | tf_op jit(solution)/shard_map/concatenate | solution.py:43
  168.0 0.0 reduce-scatter.2.cloned.1.call-update
  168.1 0.0 all-gather.5.cloned.1.call-start
  168.1 163.0 %reduce-scatter.2.cloned.1.call-done = bf16[256,3584]{0,1:T(8,128)(2,1)} async-done(((bf16[2048,3584]{0,1:T(8,128)(2,1)}), bf16[256,3584]{0,1:T(8,128)(2,1)}) %reduce-scatter.2.cloned.1.call-update) | async-done | bytes 1835024 | tf_op jit(solution)/shard_map/reduce_scatter | solution.py:42
  331.1 1.8 convert_element_type.23
  332.9 1.2 fusion.5
  334.2 0.0 all-gather.5.cloned.1.call-update
  334.2 66.2 %all-gather.5.cloned.1.call-done = bf16[2048,896]{0,1:T(8,128)(2,1)} async-done(((bf16[256,896]{0,1:T(8,128)(2,1)}), bf16[2048,896]{0,1:T(8,128)(2,1)}) %all-gather.5.cloned.1.call-update) | async-done | bytes 3670032 | tf_op jit(solution)/shard_map/all_gather | solution.py:57
  400.3 0.0 copy-start.1
  400.3 9.8 %convolution_multiply_fusion = f32[1024,896]{1,0:T(8,128)} fusion(bf16[2048,1024]{1,0:T(8,128)(2,1)} %copy-done.3, bf16[2048,896]{0,1:T(8,128)(2,1)} %all-gather.5.cloned.1.call-done), kind=kOutput, calls=%fused_computation.9 | convolution fusion | flops 3759013888 | bytes 11534336 | tf_op jit(solution)/shard_map/dot_general | solution.py:55
  410.2 0.0 copy-done.1
  (1 shorter events, 0.0 us)
Async XLA Ops:
  6.5 106.8 %copy-start = (bf16[1024,896]{1,0:T(8,128)(2,1)S(1)}, bf16[1024,896]{1,0:T(8,128)(2,1)}, u32[]{:S(2)}) copy-start(bf16[1024,896]{1,0:T(8,128)(2,1)} %param.13) | copy-start | bytes 5505028
  6.5 123.3 %all-gather.3.cloned.1.call-start = ((), (), s32[]{:S(2)}) async-start(), calls=%async_computation.2 | async-start | bytes 4456448 | tf_op jit(solution)/shard_map/all_gather | solution.py:24
  7.3 323.9 %reduce-scatter.2.cloned.1.call-start = ((), (), s32[]{:S(2)}) async-start(), calls=%async_computation.3 | async-start | bytes 16515072 | tf_op jit(solution)/shard_map/reduce_scatter | solution.py:42
  83.1 2.0 copy-start.2
  85.1 25.5 %copy-start.7 = (f32[1024]{0:T(1024)S(1)}, f32[1024]{0:T(1024)}, u32[]{:S(2)}) copy-start(f32[1024]{0:T(1024)} %param.9) | copy-start | bytes 12292
  113.4 11.0 %copy-start.3 = (bf16[2048,1024]{1,0:T(8,128)(2,1)}, bf16[2048,1024]{1,0:T(8,128)(2,1)S(1)}, u32[]{:S(2)}) copy-start(bf16[2048,1024]{1,0:T(8,128)(2,1)S(1)} %fusion.1) | copy-start | bytes 12582916
  113.4 5.5 %copy-start.8 = (bf16[1024,896]{1,0:T(8,128)(2,1)S(1)}, bf16[1024,896]{1,0:T(8,128)(2,1)}, u32[]{:S(2)}) copy-start(bf16[1024,896]{1,0:T(8,128)(2,1)} %param.11) | copy-start | bytes 5505028
  118.9 5.5 %copy-start.9 = (bf16[1024,896]{1,0:T(8,128)(2,1)S(1)}, bf16[1024,896]{1,0:T(8,128)(2,1)}, u32[]{:S(2)}) copy-start(bf16[1024,896]{1,0:T(8,128)(2,1)} %param.10) | copy-start | bytes 5505028
  129.8 6.9 %copy-start.4 = (bf16[2048,896]{0,1:T(8,128)(2,1)S(1)}, bf16[2048,896]{0,1:T(8,128)(2,1)}, u32[]{:S(2)}) copy-start(bf16[2048,896]{0,1:T(8,128)(2,1)} %convolution_convert_fusion.1) | copy-start | bytes 11010052
  129.8 6.9 %copy-start.5 = (bf16[2048,896]{0,1:T(8,128)(2,1)S(1)}, bf16[2048,896]{0,1:T(8,128)(2,1)}, u32[]{:S(2)}) copy-start(bf16[2048,896]{0,1:T(8,128)(2,1)} %convolution_convert_fusion.2) | copy-start | bytes 11010052
  129.9 6.9 %copy-start.6 = (bf16[2048,896]{0,1:T(8,128)(2,1)S(1)}, bf16[2048,896]{0,1:T(8,128)(2,1)}, u32[]{:S(2)}) copy-start(bf16[2048,896]{0,1:T(8,128)(2,1)} %convolution_convert_fusion.3) | copy-start | bytes 11010052
  168.1 232.3 %all-gather.5.cloned.1.call-start = ((), (), s32[]{:S(2)}) async-start(), calls=%async_computation.4 | async-start | bytes 4128768 | tf_op jit(solution)/shard_map/all_gather | solution.py:57
  400.3 9.8 %copy-start.1 = (bf16[1024,896]{1,0:T(8,128)(2,1)S(1)}, bf16[1024,896]{1,0:T(8,128)(2,1)}, u32[]{:S(2)}) copy-start(bf16[1024,896]{1,0:T(8,128)(2,1)} %param.13) | copy-start | bytes 5505028
Sparse Core Ops, SparseCore 0:
  9.0 76.2 all-gather.2
  168.2 162.9 reduce-scatter.1
  334.3 65.9 all-gather.4
